TPU v7x, 256 devices: a whole 4x4x8 slice. The times are simulated.
256 devices in a mesh: seq: 64 (over z, y, core), tp: 4 (over x).
Axes of the slice: x: 4, y: 4, z: 8, core: 2. Of those that a mesh axis runs over, the one named last changes fastest.
Arguments:
- db_tokens: int32 [32768, 128], P('seq'), may hold values from 0 to 16383
- db_parent: int32 [32768, 128], P('seq'), may hold values from 0 to 126, as said below
- db_depth: int32 [32768, 128], P('seq'), may hold values from 0 to 31, as said below
- nb_rows: int32 [512, 2], P('seq'), may hold values from 0 to 32767, as said below
- seq_start: int32 [512], P('seq'), may hold values 0 or 1
- table: bfloat16 [16384, 1024], P(None, 'tp'), may hold values from -40 to 40
- depth_table: bfloat16 [32, 1024], P(None, 'tp'), may hold values from -3 to 3
- enc_gain: float32 [1024], replicated, may hold values from 0.25 to 1.75
- enc_qkv: bfloat16 [1024, 3, 1024], P('seq', None, 'tp'), may hold values from -0.1875 to 0.1875
- tree_bias: float32 [8], replicated, may hold values from 1 to 4
- enc_wo: bfloat16 [1024, 1024], P('tp', 'seq'), may hold values from -0.1875 to 0.1875
- cond_kv: bfloat16 [32768, 2, 1024], P('seq', None, 'tp'), may hold values from -150 to 150
- queries: bfloat16 [32768, 4096], P('seq', 'tp'), may hold values from -150 to 150
- cca_kv: bfloat16 [1024, 2, 512], P('seq', None, 'tp'), may hold values from -0.1875 to 0.1875
Outputs:
- attended: bfloat16 [32768, 4096], P('seq', 'tp')
Inputs may be any that keep to these rules, and one draw needn't show every extreme that they name: `db_parent`: position 0 of every stored neighbour is its own parent; every other position's parent is one of the three positions just before it. `db_depth`: position 0 has depth 0; every other position has its parent's depth plus one, capped at 31. `nb_rows`: rows 512 * i to 512 * (i + 1) - 1 of the database lie on index i of seq. Of the 16 neighbours of one index's blocks at most 1 lie on any one index; at most 32 neighbours of all blocks lie on one index, and in every draw some index holds exactly 32.
All inputs are finite; a program needn't handle non-finite values. No bound on the sum of `seq_start` on one device may be relied on, other than what follows from the above.
Results may differ from a plain program's by a relative error of at most 0.0223.
The roundings to bfloat16 on the way count: a program that leaves them out, or rounds other values in their place, can miss the bound.
Values may be sent and summed in bfloat16 or wider, within the bound.
No kernel may reach another device: no remote copies, remote signals or barrier semaphores. Data moves between devices by JAX's collectives and lax.ppermute only.
A program may use at most 128 MiB of HBM per device.

v0:
```python
import math
import jax
import jax.numpy as jnp
from jax import lax
from jax.sharding import PartitionSpec as P

HD = 128


def from_behind(value, axis, steps):
    count = lax.axis_size(axis)
    initial, last = (max(0, -steps), min(count, count - steps))
    return lax.ppermute(value, axis, [(source, source + steps) for source in range(initial, last)])


def normalize(embedded, gain):
    embedded_f = embedded.astype(jnp.float32)
    return (
        embedded_f
        * lax.rsqrt(jnp.mean(embedded_f * embedded_f, axis=-1, keepdims=True) + 1e-05)
        * gain
    ).astype(jnp.bfloat16)


def encoder_mix(normed, parents, conditioning, w_qkv, bias, head_count):
    unit_count = normed.shape[0]
    length = normed.shape[1]
    blocks = conditioning.shape[0]
    pair_count = unit_count // blocks
    cond_len = conditioning.shape[1]
    score_scale = 1.0 / math.sqrt(HD)
    projected = jnp.einsum(
        "une,eaf->unaf", normed, w_qkv, preferred_element_type=jnp.float32
    ).astype(jnp.bfloat16)
    shaped = projected.reshape(blocks, pair_count, length, 3, head_count, HD)
    query_part = shaped[:, :, :, 0]
    key_part = shaped[:, :, :, 1]
    value_part = shaped[:, :, :, 2]
    cond_keys = conditioning[:, :, 0].reshape(blocks, cond_len, head_count, HD)
    cond_values = conditioning[:, :, 1].reshape(blocks, cond_len, head_count, HD)
    self_scores = (
        jnp.einsum("cpihd,cpjhd->cphij", query_part, key_part, preferred_element_type=jnp.float32)
        * score_scale
    )
    parent_hit = (
        parents.reshape(blocks, pair_count, length)[:, :, :, None]
        == jnp.arange(length, dtype=jnp.float32)[None, None, None, :]
    ).astype(jnp.float32)
    self_scores = self_scores + bias[None, None, :, None, None] * parent_hit[:, :, None]
    cond_scores = (
        jnp.einsum("cpihd,crhd->cphir", query_part, cond_keys, preferred_element_type=jnp.float32)
        * score_scale
    )
    weights = jax.nn.softmax(jnp.concatenate([self_scores, cond_scores], axis=-1), axis=-1).astype(
        jnp.bfloat16
    )
    mixed = jnp.einsum(
        "cphij,cpjhd->cpihd", weights[..., :length], value_part, preferred_element_type=jnp.float32
    )
    mixed = mixed + jnp.einsum(
        "cphir,crhd->cpihd", weights[..., length:], cond_values, preferred_element_type=jnp.float32
    )
    return mixed.astype(jnp.bfloat16).reshape(unit_count, length, head_count * HD)


def attend(query, key_value):
    blocks, key_rows = (key_value.shape[0], key_value.shape[1])
    token_count = query.shape[1]
    head_count = query.shape[2]
    kv_heads = key_value.shape[3] // HD
    group = head_count // kv_heads
    grouped = query.reshape(blocks, token_count, kv_heads, group, HD)
    key_part = key_value[:, :, 0].reshape(blocks, key_rows, kv_heads, HD)
    value_part = key_value[:, :, 1].reshape(blocks, key_rows, kv_heads, HD)
    scores = jnp.einsum(
        "ctkgd,cpkd->ckgtp", grouped, key_part, preferred_element_type=jnp.float32
    ) * (1.0 / math.sqrt(HD))
    weights = jax.nn.softmax(scores, axis=-1).astype(jnp.bfloat16)
    output = jnp.einsum(
        "ckgtp,cpkd->ctkgd", weights, value_part, preferred_element_type=jnp.float32
    ).astype(jnp.bfloat16)
    return output.reshape(blocks, token_count, head_count, HD)


def shards(
    db_tokens,
    db_parent,
    db_depth,
    nb_rows,
    seq_start,
    table,
    depth_table,
    enc_gain,
    enc_qkv,
    tree_bias,
    enc_wo,
    cond_kv,
    queries,
    cca_kv,
):
    seq_size = lax.axis_size("seq")
    tp_size = lax.axis_size("tp")
    block_count, pair_count = nb_rows.shape
    unit_count = block_count * pair_count
    stored = db_tokens.shape[0]
    length = db_tokens.shape[1]
    slot_count = max(1, 2 * unit_count // seq_size)
    flat_rows = nb_rows.reshape(unit_count)
    holder = flat_rows // stored
    local_row = flat_rows % stored
    ordering = jnp.arange(unit_count, dtype=jnp.int32)
    earlier = jnp.sum(
        ((holder[:, None] == holder[None, :]) & (ordering[:, None] > ordering[None, :])).astype(
            jnp.int32
        ),
        axis=1,
    )
    target = holder * slot_count + earlier
    places = jnp.arange(seq_size * slot_count, dtype=jnp.int32)
    request = jnp.sum(
        jnp.where(target[None, :] == places[:, None], local_row[None, :], 0), axis=1
    ).reshape(seq_size, slot_count)
    wanted = lax.all_to_all(request, "seq", split_axis=0, concat_axis=0, tiled=True)
    tokens = jnp.take(db_tokens, wanted, axis=0)
    depths = jnp.take(db_depth, wanted, axis=0)
    parents = jnp.take(db_parent, wanted, axis=0).astype(jnp.bfloat16)
    embedded = (
        jnp.take(table, tokens, axis=0).astype(jnp.float32)
        + jnp.take(depth_table, depths, axis=0).astype(jnp.float32)
    ).astype(jnp.bfloat16)
    fetched = lax.all_to_all(embedded, "seq", split_axis=0, concat_axis=0, tiled=True)
    fetched_parents = lax.all_to_all(parents, "seq", split_axis=0, concat_axis=0, tiled=True)
    embedded = jnp.take(
        fetched.reshape((seq_size * slot_count,) + fetched.shape[2:]), target, axis=0
    )
    parents = jnp.take(
        fetched_parents.reshape(seq_size * slot_count, length), target, axis=0
    ).astype(jnp.float32)
    row_qkv, row_out = (
        lax.all_gather(enc_qkv, "seq", axis=0, tiled=True),
        lax.all_gather(enc_wo, "seq", axis=1, tiled=True),
    )
    cond_columns = cond_kv.shape[2]
    cond_len = cond_kv.shape[0] // block_count
    full_width = row_qkv.shape[0]
    head_count = row_qkv.shape[2] // HD
    conditioning = cond_kv.reshape(block_count, cond_len, 2, cond_columns)
    gathered = lax.all_gather(embedded, "tp", axis=2, tiled=True)
    normed = normalize(gathered, enc_gain)
    bias_here = lax.dynamic_slice_in_dim(tree_bias, lax.axis_index("tp") * head_count, head_count)
    mixed = encoder_mix(normed, parents, conditioning, row_qkv, bias_here, head_count).reshape(
        unit_count * length, head_count * HD
    )
    row_share = unit_count * length // tp_size
    increment = lax.psum_scatter(
        jnp.dot(mixed, row_out, preferred_element_type=jnp.float32),
        "tp",
        scatter_dimension=0,
        tiled=True,
    )
    residual = lax.dynamic_slice_in_dim(
        gathered.reshape(unit_count * length, full_width),
        lax.axis_index("tp") * row_share,
        row_share,
        0,
    )
    encoded_part = (residual.astype(jnp.float32) + increment).astype(jnp.bfloat16)
    encoded = lax.all_gather(encoded_part, "tp", axis=0, tiled=True)
    kv_weight = lax.all_gather(cca_kv, "seq", axis=0, tiled=True)
    key_rows = pair_count * length
    keys_values = jnp.einsum(
        "re,eaf->raf", encoded, kv_weight, preferred_element_type=jnp.float32
    ).astype(jnp.bfloat16)
    keys_values = keys_values.reshape(block_count, key_rows, 2, keys_values.shape[2])
    carried = from_behind(keys_values[block_count - 1], "seq", 1)
    previous = jnp.concatenate([carried[None], keys_values[: block_count - 1]], axis=0)
    head_queries = queries.shape[1] // HD
    query_heads = queries.reshape(block_count, cond_len, head_queries, HD)
    leading = attend(query_heads[:, : cond_len - 1], previous)
    trailing = attend(query_heads[:, cond_len - 1 :], keys_values)
    block_index = lax.axis_index("seq") * block_count + jnp.arange(block_count, dtype=jnp.int32)
    allowed = (block_index > 0) & (seq_start == 0)
    leading = jnp.where(allowed[:, None, None, None], leading, jnp.zeros_like(leading))
    attended = jnp.concatenate([leading, trailing], axis=1)
    return attended.reshape(block_count * cond_len, head_queries * HD)


def solution(mesh):
    in_specs = (
        P("seq", None),
        P("seq", None),
        P("seq", None),
        P("seq", None),
        P("seq"),
        P(None, "tp"),
        P(None, "tp"),
        P(),
        P("seq", None, "tp"),
        P(),
        P("tp", "seq"),
        P("seq", None, "tp"),
        P("seq", "tp"),
        P("seq", None, "tp"),
    )
    out_specs = P("seq", "tp")
    return jax.shard_map(shards, mesh=mesh, in_specs=in_specs, out_specs=out_specs, check_vma=False)
```

profile of v0, /device:TPU:128, one launch (start us, length us, event | category | flops | bytes accessed | tf_op | source)
XLA Modules:
  0.0 528.6 jit_solution(15645028171673913726)
XLA Ops:
  6.5 0.8 copy.109
  7.8 15.1 %all_to_all.22 = s32[64,1,1]{2,1,0:T(1,128)S(1)} all-to-all(s32[64,1,1]{2,1,0:T(1,128)S(1)} %copy.110), channel_id=1, replica_groups=mesh['seq'=64,'tp'=4] {'seq'}, dimensions={0} | all-to-all | bytes 512 | tf_op jit(solution)/shard_map/all_to_all | solution.py:123
  22.9 1.2 reduce.6
  24.2 0.6 gather_fusion.4
  24.8 1.5 gather_fusion.5
  26.6 33.1 %gather_fusion.1 = bf16[8192,256]{1,0:T(8,128)(2,1)} fusion(bf16[32,256]{1,0:T(8,128)(2,1)S(1)} %copy-done.2, s32[8192]{0:T(1024)S(1)} %get-tuple-element.16), kind=kCustom, calls=%fused_computation.4 | custom fusion | bytes 8421376 | tf_op jit(solution)/shard_map/jit(_take)/gather | solution.py:129
  59.7 35.5 %gather_fusion = bf16[8192,256]{1,0:T(8,128)(2,1)} fusion(bf16[16384,256]{1,0:T(8,128)(2,1)} %param.21, s32[8192]{0:T(1024)S(1)} %get-tuple-element.15), kind=kCustom, calls=%fused_computation.3 | custom fusion | bytes 8421376 | tf_op jit(solution)/shard_map/jit(_take)/gather | solution.py:128
  95.2 8.5 %add_convert_fusion = bf16[64,1,128,256]{3,2,1,0:T(8,128)(2,1)} fusion(bf16[64,1,128,256]{3,2,1,0:T(8,128)(2,1)} %bitcast.204, bf16[64,1,128,256]{3,2,1,0:T(8,128)(2,1)} %bitcast.205, pred[64,128]{1,0:T(8,128)(4,1)S(1)} %get-tuple-element.14, pred[64,128]{1,0:T(8,128)(4,1)S(1)} %get-tuple-element.13), kind=kLoop, calls=%fused_computation.12 | loop fusion | flops 12582912 | bytes 12599296 | tf_op jit(solution)/shard_map/convert_element_type | solution.py:130
  103.7 10.4 %all-to-all-start.1 = ((bf16[64,1,128,256]{3,2,1,0:T(8,128)(2,1)}), bf16[64,1,128,256]{3,2,1,0:T(8,128)(2,1)}, u32[]{:S(2)}, u32[]{:S(2)}) async-start(bf16[64,1,128,256]{3,2,1,0:T(8,128)(2,1)} %add_convert_fusion), calls=%async_computation.1 | async-start | bytes 8388608 | tf_op jit(solution)/shard_map/all_to_all | solution.py:131
  114.3 91.3 %all-to-all-done.1 = bf16[64,1,128,256]{3,2,1,0:T(8,128)(2,1)} async-done(((bf16[64,1,128,256]{3,2,1,0:T(8,128)(2,1)}), bf16[64,1,128,256]{3,2,1,0:T(8,128)(2,1)}, u32[]{:S(2)}, u32[]{:S(2)}) %all-to-all-start.1) | async-done | bytes 4194336 | tf_op jit(solution)/shard_map/all_to_all | solution.py:131
  205.6 2.8 gather_fusion.2
  208.4 1.1 broadcast_select_fusion
  209.6 0.7 all-gather.6.cloned.1.call-update
  210.5 2.2 slice_reduce_fusion
  212.6 0.6 gather_fusion.6
  213.3 0.6 copy.121
  214.0 10.0 %all-to-all-start.2 = ((bf16[64,1,128]{2,1,0:T(2,128)(2,1)}), bf16[64,1,128]{2,1,0:T(2,128)(2,1)S(1)}, u32[]{:S(2)}, u32[]{:S(2)}) async-start(bf16[64,1,128]{2,1,0:T(2,128)(2,1)} %copy.121), calls=%async_computation.2 | async-start | bytes 65536 | tf_op jit(solution)/shard_map/all_to_all | solution.py:132
  224.1 54.2 %all_gather.17 = bf16[256,1024]{0,1:T(8,128)(2,1)} all-gather(bf16[256,16]{0,1:T(8,128)(2,1)S(1)} %copy-done.10), channel_id=1, replica_groups=mesh['seq'=64,'tp'=4] {'seq'}, dimensions={1}, use_global_device_ids=true | all-gather | bytes 532480 | tf_op jit(solution)/shard_map/all_gather | solution.py:141
  278.3 0.8 reshape_squeeze.7
  279.2 0.6 gather_fusion.3
  279.9 1.1 fusion.45
  281.0 3.1 fusion
  284.1 53.3 %all-gather.6.cloned.1.call-done = bf16[1024,3,256]{2,0,1:T(8,128)(2,1)} async-done(((bf16[16,3,256]{2,0,1:T(8,128)(2,1)}), bf16[1024,3,256]{2,0,1:T(8,128)(2,1)}) %all-gather.6.cloned.1.call-update) | async-done | bytes 1572880 | tf_op jit(solution)/shard_map/all_gather | solution.py:140
  337.4 7.9 %fusion.16 = bf16[16,128,3,256]{3,1,2,0:T(8,128)(2,1)} fusion(bf16[16,128,1024]{2,1,0:T(8,128)(2,1)} %all-gather.4.cloned.1.call-done, f32[1024]{0:T(1024)S(1)} %copy-done.12, f32[16,128]{1,0:T(8,128)S(1)} %add_rsqrt_fusion, bf16[1024,3,256]{2,0,1:T(8,128)(2,1)} %all-gather.6.cloned.1.call-done), kind=kOutput, calls=%fused_computation.28 | convolution fusion | flops 3231186944 | bytes 8925184 | tf_op jit(solution)/shard_map/une,eaf->unaf/dot_general | solution.py:32
  345.3 3.8 reshape.389
  349.0 3.2 fusion.69
  352.2 0.5 fusion.71
  352.7 0.9 fusion.70
  353.6 0.6 fusion.19
  354.2 0.6 divide_convert_fusion.1
  354.8 1.9 copy.150
  356.8 1.7 fusion.40
  358.5 0.5 fusion.22
  359.0 0.8 copy.130
  359.8 4.5 fusion.37
  364.4 84.3 %reduce-scatter.2.cloned.1.call-done = f32[512,1024]{1,0:T(8,128)} async-done(((f32[2048,1024]{1,0:T(8,128)}), f32[512,1024]{1,0:T(8,128)}) %reduce-scatter.2.cloned.1.call-update) | async-done | bytes 2097168 | tf_op jit(solution)/shard_map/reduce_scatter | solution.py:155
  448.7 3.2 add_convert_fusion.1
  452.3 43.8 %all_gather.19 = bf16[1024,2,128]{2,0,1:T(8,128)(2,1)S(1)} all-gather(bf16[16,2,128]{2,0,1:T(8,128)(2,1)S(1)} %copy.131), channel_id=1, replica_groups=mesh['seq'=64,'tp'=4] {'seq'}, dimensions={0}, use_global_device_ids=true | all-gather | bytes 532480 | tf_op jit(solution)/shard_map/all_gather | solution.py:169
  496.2 6.5 %all-gather.8.cloned.1.call-done = bf16[2048,1024]{1,0:T(8,128)(2,1)} async-done(((bf16[512,1024]{1,0:T(8,128)(2,1)}), bf16[2048,1024]{1,0:T(8,128)(2,1)}) %all-gather.8.cloned.1.call-update) | async-done | bytes 4194320 | tf_op jit(solution)/shard_map/all_gather | solution.py:168
  502.6 3.4 fusion.13
  506.1 1.9 collective-permute-start
  508.1 0.3 fusion.72
  508.8 6.9 %collective-permute-done = bf16[256,2,128]{2,0,1:T(8,128)(2,1)S(1)} collective-permute-done((bf16[256,2,128]{2,0,1:T(8,128)(2,1)S(1)}, bf16[256,2,128]{2,0,1:T(8,128)(2,1)S(1)}, u32[]{:S(2)}, u32[]{:S(2)}) %collective-permute-start) | collective-permute-done | bytes 131104 | tf_op jit(solution)/shard_map/ppermute | solution.py:13
  515.7 0.8 bitcast_reduce_fusion
  516.5 1.4 fusion.11
  518.0 1.9 fusion.34
  520.1 0.7 copy.135
  520.8 1.2 copy.186
  (72 shorter events, 2.6 us)
Async XLA Ops:
  6.5 17.7 %copy-start = (s32[512,128]{1,0:T(8,128)S(1)}, s32[512,128]{1,0:T(8,128)}, u32[]{:S(2)}) copy-start(s32[512,128]{1,0:T(8,128)} %param.16) | copy-start | bytes 786436
  6.5 20.0 %copy-start.2 = (bf16[32,256]{1,0:T(8,128)(2,1)S(1)}, bf16[32,256]{1,0:T(8,128)(2,1)}, u32[]{:S(2)}) copy-start(bf16[32,256]{1,0:T(8,128)(2,1)} %param.22) | copy-start | bytes 49156
  103.7 101.9 %all-to-all-start.1 = ((bf16[64,1,128,256]{3,2,1,0:T(8,128)(2,1)}), bf16[64,1,128,256]{3,2,1,0:T(8,128)(2,1)}, u32[]{:S(2)}, u32[]{:S(2)}) async-start(bf16[64,1,128,256]{3,2,1,0:T(8,128)(2,1)} %add_convert_fusion), calls=%async_computation.1 | async-start | bytes 8388608 | tf_op jit(solution)/shard_map/all_to_all | solution.py:131
  114.1 96.3 %copy-start.6 = (bf16[512,2,256]{2,1,0:T(2,128)(2,1)S(1)}, bf16[512,2,256]{2,1,0:T(2,128)(2,1)}, u32[]{:S(2)}) copy-start(bf16[512,2,256]{2,1,0:T(2,128)(2,1)} %param.27) | copy-start | bytes 1572868
  114.1 98.5 %copy-start.9 = (s32[512,128]{1,0:T(8,128)S(1)}, s32[512,128]{1,0:T(8,128)}, u32[]{:S(2)}) copy-start(s32[512,128]{1,0:T(8,128)} %param.17) | copy-start | bytes 786436
  114.1 109.9 %copy-start.10 = (bf16[256,16]{0,1:T(8,128)(2,1)S(1)}, bf16[256,16]{0,1:T(8,128)(2,1)}, u32[]{:S(2)}) copy-start(bf16[256,16]{0,1:T(8,128)(2,1)} %param.26) | copy-start | bytes 24580
  114.2 166.8 %all-gather.4.cloned.1.call-start = ((), (), s32[]{:S(2)}) async-start(), calls=%async_computation.4 | async-start | bytes 5242880 | tf_op jit(solution)/shard_map/all_gather | solution.py:148
  205.6 73.5 %copy-start.13 = (f32[8]{0:T(128)S(1)}, f32[8]{0:T(128)}, u32[]{:S(2)}) copy-start(f32[8]{0:T(128)} %param.25) | copy-start | bytes 100
  209.6 127.8 %all-gather.6.cloned.1.call-start = ((), (), s32[]{:S(2)}) async-start(), calls=%async_computation.5 | async-start | bytes 1597440 | tf_op jit(solution)/shard_map/all_gather | solution.py:140
  210.4 126.9 %copy-start.12 = (f32[1024]{0:T(1024)S(1)}, f32[1024]{0:T(1024)}, u32[]{:S(2)}) copy-start(f32[1024]{0:T(1024)} %param.23) | copy-start | bytes 12292
  214.0 65.2 %all-to-all-start.2 = ((bf16[64,1,128]{2,1,0:T(2,128)(2,1)}), bf16[64,1,128]{2,1,0:T(2,128)(2,1)S(1)}, u32[]{:S(2)}, u32[]{:S(2)}) async-start(bf16[64,1,128]{2,1,0:T(2,128)(2,1)} %copy.121), calls=%async_computation.2 | async-start | bytes 65536 | tf_op jit(solution)/shard_map/all_to_all | solution.py:132
  224.0 224.7 %reduce-scatter.2.cloned.1.call-start = ((), (), s32[]{:S(2)}) async-start(), calls=%async_computation.6 | async-start | bytes 10485760 | tf_op jit(solution)/shard_map/reduce_scatter | solution.py:155
  349.0 3.7 copy-start.3
  353.6 1.2 copy-start.4
  354.8 3.7 copy-start.8
  356.8 3.0 copy-start.5
  364.3 87.6 %copy-start.11 = (bf16[16,2,128]{2,1,0:T(2,128)(2,1)S(1)}, bf16[16,2,128]{2,1,0:T(2,128)(2,1)}, u32[]{:S(2)}) copy-start(bf16[16,2,128]{2,1,0:T(2,128)(2,1)} %param.29) | copy-start | bytes 24580
  364.3 87.6 %copy-start.7 = (bf16[512,1024]{1,0:T(8,128)(2,1)S(1)}, bf16[512,1024]{1,0:T(8,128)(2,1)}, u32[]{:S(2)}) copy-start(bf16[512,1024]{1,0:T(8,128)(2,1)} %param.28) | copy-start | bytes 3145732
  364.4 138.2 %all-gather.8.cloned.1.call-start = ((), (), s32[]{:S(2)}) async-start(), calls=%async_computation.7 | async-start | bytes 5242880 | tf_op jit(solution)/shard_map/all_gather | solution.py:168
  448.7 47.4 %copy-start.14 = (s32[8]{0:T(128)S(1)}, s32[8]{0:T(128)}, u32[]{:S(2)}) copy-start(s32[8]{0:T(128)} %param.20) | copy-start | bytes 100
  506.1 9.6 %collective-permute-start = (bf16[256,2,128]{2,0,1:T(8,128)(2,1)S(1)}, bf16[256,2,128]{2,0,1:T(8,128)(2,1)S(1)}, u32[]{:S(2)}, u32[]{:S(2)}) collective-permute-start(bf16[256,2,128]{2,0,1:T(8,128)(2,1)S(1)} %slice.86), channel_id=1, source_target_pairs={{0,4},{4,8},{8,12},{12,16},{16,20},{20,24},{24,28},{28,32},{32,36}... | collective-permute-start | bytes 393224 | tf_op jit(solution)/shard_map/ppermute | solution.py:13
  518.0 4.0 copy-start.1
Sparse Core Ops, SparseCore 0:
  209.7 54.9 all-gather.3
  267.3 69.9 all-gather.5
  364.5 84.2 reduce-scatter.1
  452.1 50.4 all-gather.7
where the time goes:
time: 529 us
  waiting for transfers between devices  243 us (46%)
  blocking collectives  113 us (21%)
  local copies, waits for them, and re-layouts  91.8 us (17%)
  matrix products  22.6 us (4%)
  starting transfers between devices  22.5 us (4%)
  other arithmetic  21.9 us (4%)
  between operations  13.6 us (3%)
    all_to_all x1, waiting for transfers between devices, shards(): lax.all_to_all(embedded, 'seq', split_axis=0, concat_axis=0, tiled=True)  91.3 us
    reduce_scatter x1, waiting for transfers between devices, shards(): lax.psum_scatter(jnp.dot(mixed, row_out, preferred_element_type=jnp.float...  84.3 us
    all_gather x1, blocking collectives, shards(): lax.all_gather(enc_wo, 'seq', axis=1, tiled=True)  54.2 us
    all_gather x1, waiting for transfers between devices, shards(): lax.all_gather(enc_qkv, 'seq', axis=0, tiled=True)  53.3 us
    all_gather x1, blocking collectives, shards(): kv_weight = lax.all_gather(cca_kv, 'seq', axis=0, tiled=True)  43.8 us
    gather x1, local copies, waits for them, and re-layouts, shards(): jnp.take(table, tokens, axis=0).astype(jnp.float32)  35.5 us
    gather x1, local copies, waits for them, and re-layouts, shards(): jnp.take(depth_table, depths, axis=0).astype(jnp.float32)  33.1 us
    all_to_all x1, blocking collectives, shards(): lax.all_to_all(request, 'seq', split_axis=0, concat_axis=0, tiled=True)  15.1 us
  transfers between devices with their start and end apart: 7, of which 5 were waited for; matrix products, arithmetic and copies ran while one was open for 2% of the time, Pallas kernels for 0%

commit v1 on v0

--- a/solution.py
+++ b/solution.py
@@ -137,7 +137,9 @@
         fetched_parents.reshape(seq_size * slot_count, length), target, axis=0
     ).astype(jnp.float32)
     row_qkv, row_out = (
-        lax.all_gather(enc_qkv, "seq", axis=0, tiled=True),
+        jnp.concatenate(
+            lax.all_to_all(jnp.stack([enc_qkv] * lax.axis_size("seq")), "seq", 0, 0), axis=0
+        ),
         lax.all_gather(enc_wo, "seq", axis=1, tiled=True),
     )
     cond_columns = cond_kv.shape[2]

time: 529 us -> 512 us (0.968)
  waiting for transfers between devices: 243 us -> 188 us
  blocking collectives: 113 us -> 154 us
    all_gather x1 -> x0, waiting for transfers between devices: 53.3 us -> none  [shards(): lax.all_gather(enc_qkv, 'seq', axis=0, tiled=True)]
    all_gather x1, blocking collectives: 54.2 us -> 79.7 us  [shards(): lax.all_gather(enc_wo, 'seq', axis=1, tiled=True)]
    all_to_all x0 -> x1, blocking collectives: none -> 14.7 us  [shards(): lax.all_to_all(parents, 'seq', split_axis=0, concat_axis=0, tiled=True)]
  transfers between devices with their start and end apart: 7 -> 6, of which waited for: 5 -> 4; matrix products, arithmetic and copies ran while one was open for 2% -> 2% of each run, Pallas kernels for 0% -> 0%
where the time goes in v1:
time: 512 us
  waiting for transfers between devices  188 us (37%)
  blocking collectives  154 us (30%)
  local copies, waits for them, and re-layouts  92.5 us (18%)
  other arithmetic  22 us (4%)
  starting transfers between devices  21.9 us (4%)
  matrix products  19.7 us (4%)
  between operations  13.6 us (3%)
    all_to_all x1, waiting for transfers between devices, shards(): lax.all_to_all(embedded, 'seq', split_axis=0, concat_axis=0, tiled=True)  91.3 us
    reduce_scatter x1, waiting for transfers between devices, shards(): lax.psum_scatter(jnp.dot(mixed, row_out, preferred_element_type=jnp.float...  83.9 us
    all_gather x1, blocking collectives, shards(): lax.all_gather(enc_wo, 'seq', axis=1, tiled=True)  79.7 us
    all_gather x1, blocking collectives, shards(): kv_weight = lax.all_gather(cca_kv, 'seq', axis=0, tiled=True)  44 us
    gather x1, local copies, waits for them, and re-layouts, shards(): jnp.take(table, tokens, axis=0).astype(jnp.float32)  35.4 us
    gather x1, local copies, waits for them, and re-layouts, shards(): jnp.take(depth_table, depths, axis=0).astype(jnp.float32)  32.9 us
    all_to_all x1, blocking collectives, shards(): lax.all_to_all(request, 'seq', split_axis=0, concat_axis=0, tiled=True)  15.1 us
    all_to_all x1, blocking collectives, shards(): lax.all_to_all(parents, 'seq', split_axis=0, concat_axis=0, tiled=True)  14.7 us
  transfers between devices with their start and end apart: 6, of which 4 were waited for; matrix products, arithmetic and copies ran while one was open for 2% of the time, Pallas kernels for 0%

profile of v1, /device:TPU:128, one launch (start us, length us, event | category | flops | bytes accessed | tf_op | source)
XLA Modules:
  0.0 511.6 jit_solution(6799004804726428015)
XLA Ops:
  6.5 0.8 copy.111
  7.8 15.1 %all_to_all.27 = s32[64,1,1]{2,1,0:T(1,128)S(1)} all-to-all(s32[64,1,1]{2,1,0:T(1,128)S(1)} %copy.112), channel_id=1, replica_groups=mesh['seq'=64,'tp'=4] {'seq'}, dimensions={0} | all-to-all | bytes 512 | tf_op jit(solution)/shard_map/all_to_all | solution.py:123
  22.9 1.2 reduce.6
  24.2 0.6 gather_fusion.4
  24.8 1.5 gather_fusion.5
  26.6 32.9 %gather_fusion.1 = bf16[8192,256]{1,0:T(8,128)(2,1)} fusion(bf16[32,256]{1,0:T(8,128)(2,1)S(1)} %copy-done.2, s32[8192]{0:T(1024)S(1)} %get-tuple-element.16), kind=kCustom, calls=%fused_computation.4 | custom fusion | bytes 8421376 | tf_op jit(solution)/shard_map/jit(_take)/gather | solution.py:129
  59.5 35.4 %gather_fusion = bf16[8192,256]{1,0:T(8,128)(2,1)} fusion(bf16[16384,256]{1,0:T(8,128)(2,1)} %param.21, s32[8192]{0:T(1024)S(1)} %get-tuple-element.15), kind=kCustom, calls=%fused_computation.3 | custom fusion | bytes 8421376 | tf_op jit(solution)/shard_map/jit(_take)/gather | solution.py:128
  94.9 8.5 %add_convert_fusion = bf16[64,1,128,256]{3,2,1,0:T(8,128)(2,1)} fusion(bf16[64,1,128,256]{3,2,1,0:T(8,128)(2,1)} %bitcast.205, bf16[64,1,128,256]{3,2,1,0:T(8,128)(2,1)} %bitcast.206, pred[64,128]{1,0:T(8,128)(4,1)S(1)} %get-tuple-element.14, pred[64,128]{1,0:T(8,128)(4,1)S(1)} %get-tuple-element.13), kind=kLoop, calls=%fused_computation.12 | loop fusion | flops 12582912 | bytes 12599296 | tf_op jit(solution)/shard_map/convert_element_type | solution.py:130
  103.4 10.4 %all-to-all-start.1 = ((bf16[64,1,128,256]{3,2,1,0:T(8,128)(2,1)}), bf16[64,1,128,256]{3,2,1,0:T(8,128)(2,1)}, u32[]{:S(2)}, u32[]{:S(2)}) async-start(bf16[64,1,128,256]{3,2,1,0:T(8,128)(2,1)} %add_convert_fusion), calls=%async_computation.1 | async-start | bytes 8388608 | tf_op jit(solution)/shard_map/all_to_all | solution.py:131
  114.0 91.3 %all-to-all-done.1 = bf16[64,1,128,256]{3,2,1,0:T(8,128)(2,1)} async-done(((bf16[64,1,128,256]{3,2,1,0:T(8,128)(2,1)}), bf16[64,1,128,256]{3,2,1,0:T(8,128)(2,1)}, u32[]{:S(2)}, u32[]{:S(2)}) %all-to-all-start.1) | async-done | bytes 4194336 | tf_op jit(solution)/shard_map/all_to_all | solution.py:131
  205.3 2.8 gather_fusion.2
  208.1 1.1 broadcast_select_fusion
  209.3 0.6 gather_fusion.6
  210.0 14.7 %all_to_all.28 = bf16[64,1,128]{2,1,0:T(2,128)(2,1)S(1)} all-to-all(bf16[64,1,128]{2,1,0:T(2,128)(2,1)S(1)} %copy.124), channel_id=1, replica_groups=mesh['seq'=64,'tp'=4] {'seq'}, dimensions={0} | all-to-all | bytes 32768 | tf_op jit(solution)/shard_map/all_to_all | solution.py:132
  224.7 1.3 stack.2
  225.9 9.5 %all-to-all-start.2 = ((bf16[64,16,3,256]{3,1,2,0:T(8,128)(2,1)}), bf16[64,16,3,256]{3,1,2,0:T(8,128)(2,1)S(1)}, u32[]{:S(2)}, u32[]{:S(2)}) async-start(bf16[64,16,3,256]{3,1,2,0:T(8,128)(2,1)} %stack.2), calls=%async_computation.2 | async-start | bytes 3145728 | tf_op jit(solution)/shard_map/all_to_all | solution.py:141
  235.5 2.2 slice_reduce_fusion
  237.8 0.8 reshape_squeeze.7
  238.6 79.7 %all_gather.13 = bf16[256,1024]{0,1:T(8,128)(2,1)} all-gather(bf16[256,16]{0,1:T(8,128)(2,1)S(1)} %copy-done.12), channel_id=1, replica_groups=mesh['seq'=64,'tp'=4] {'seq'}, dimensions={1}, use_global_device_ids=true | all-gather | bytes 532480 | tf_op jit(solution)/shard_map/all_gather | solution.py:143
  318.4 0.6 gather_fusion.3
  319.1 1.1 fusion.44
  320.4 3.2 fusion
  323.8 4.9 fusion.16
  328.7 3.8 reshape.395
  332.5 3.2 fusion.68
  335.7 0.5 fusion.70
  336.2 0.9 fusion.69
  337.1 0.6 fusion.19
  337.7 0.6 divide_convert_fusion.1
  338.3 1.9 copy.153
  340.2 1.7 fusion.39
  341.9 0.5 fusion.22
  342.4 0.8 copy.133
  343.3 4.5 fusion.36
  347.9 83.9 %reduce-scatter.2.cloned.1.call-done = f32[512,1024]{1,0:T(8,128)} async-done(((f32[2048,1024]{1,0:T(8,128)}), f32[512,1024]{1,0:T(8,128)}) %reduce-scatter.2.cloned.1.call-update) | async-done | bytes 2097168 | tf_op jit(solution)/shard_map/reduce_scatter | solution.py:157
  431.8 3.2 add_convert_fusion.1
  435.0 0.3 copy.160
  435.4 44.0 %all_gather.15 = bf16[1024,2,128]{2,0,1:T(8,128)(2,1)S(1)} all-gather(bf16[16,2,128]{2,0,1:T(8,128)(2,1)S(1)} %copy.134), channel_id=1, replica_groups=mesh['seq'=64,'tp'=4] {'seq'}, dimensions={0}, use_global_device_ids=true | all-gather | bytes 532480 | tf_op jit(solution)/shard_map/all_gather | solution.py:171
  479.4 6.2 %all-gather.5.cloned.1.call-done = bf16[2048,1024]{1,0:T(8,128)(2,1)} async-done(((bf16[512,1024]{1,0:T(8,128)(2,1)}), bf16[2048,1024]{1,0:T(8,128)(2,1)}) %all-gather.5.cloned.1.call-update) | async-done | bytes 4194320 | tf_op jit(solution)/shard_map/all_gather | solution.py:170
  485.6 3.4 fusion.13
  489.2 1.9 collective-permute-start
  491.1 0.3 fusion.71
  491.9 6.9 %collective-permute-done = bf16[256,2,128]{2,0,1:T(8,128)(2,1)S(1)} collective-permute-done((bf16[256,2,128]{2,0,1:T(8,128)(2,1)S(1)}, bf16[256,2,128]{2,0,1:T(8,128)(2,1)S(1)}, u32[]{:S(2)}, u32[]{:S(2)}) %collective-permute-start) | collective-permute-done | bytes 131104 | tf_op jit(solution)/shard_map/ppermute | solution.py:13
  498.8 0.8 bitcast_reduce_fusion
  499.6 1.4 fusion.11
  501.0 1.9 fusion.33
  503.1 0.7 copy.138
  503.8 1.2 copy.189
  (76 shorter events, 2.7 us)
Async XLA Ops:
  6.5 17.7 %copy-start = (s32[512,128]{1,0:T(8,128)S(1)}, s32[512,128]{1,0:T(8,128)}, u32[]{:S(2)}) copy-start(s32[512,128]{1,0:T(8,128)} %param.16) | copy-start | bytes 786436
  6.5 20.0 %copy-start.2 = (bf16[32,256]{1,0:T(8,128)(2,1)S(1)}, bf16[32,256]{1,0:T(8,128)(2,1)}, u32[]{:S(2)}) copy-start(bf16[32,256]{1,0:T(8,128)(2,1)} %param.22) | copy-start | bytes 49156
  103.4 101.9 %all-to-all-start.1 = ((bf16[64,1,128,256]{3,2,1,0:T(8,128)(2,1)}), bf16[64,1,128,256]{3,2,1,0:T(8,128)(2,1)}, u32[]{:S(2)}, u32[]{:S(2)}) async-start(bf16[64,1,128,256]{3,2,1,0:T(8,128)(2,1)} %add_convert_fusion), calls=%async_computation.1 | async-start | bytes 8388608 | tf_op jit(solution)/shard_map/all_to_all | solution.py:131
  113.8 95.5 %copy-start.10 = (s32[512,128]{1,0:T(8,128)S(1)}, s32[512,128]{1,0:T(8,128)}, u32[]{:S(2)}) copy-start(s32[512,128]{1,0:T(8,128)} %param.17) | copy-start | bytes 786436
  113.8 110.9 %copy-start.11 = (bf16[16,3,256]{2,0,1:T(8,128)(2,1)S(1)}, bf16[16,3,256]{2,0,1:T(8,128)(2,1)}, u32[]{:S(2)}) copy-start(bf16[16,3,256]{2,0,1:T(8,128)(2,1)} %param.24) | copy-start | bytes 73732
  113.8 206.5 %all-gather.3.cloned.1.call-start = ((), (), s32[]{:S(2)}) async-start(), calls=%async_computation.5 | async-start | bytes 5242880 | tf_op jit(solution)/shard_map/all_gather | solution.py:150
  208.1 27.4 %copy-start.7 = (bf16[512,2,256]{2,1,0:T(2,128)(2,1)S(1)}, bf16[512,2,256]{2,1,0:T(2,128)(2,1)}, u32[]{:S(2)}) copy-start(bf16[512,2,256]{2,1,0:T(2,128)(2,1)} %param.27) | copy-start | bytes 1572868
  209.2 29.3 %copy-start.15 = (f32[8]{0:T(128)S(1)}, f32[8]{0:T(128)}, u32[]{:S(2)}) copy-start(f32[8]{0:T(128)} %param.25) | copy-start | bytes 100
  209.2 29.4 %copy-start.12 = (bf16[256,16]{0,1:T(8,128)(2,1)S(1)}, bf16[256,16]{0,1:T(8,128)(2,1)}, u32[]{:S(2)}) copy-start(bf16[256,16]{0,1:T(8,128)(2,1)} %param.26) | copy-start | bytes 24580
  225.9 94.2 %all-to-all-start.2 = ((bf16[64,16,3,256]{3,1,2,0:T(8,128)(2,1)}), bf16[64,16,3,256]{3,1,2,0:T(8,128)(2,1)S(1)}, u32[]{:S(2)}, u32[]{:S(2)}) async-start(bf16[64,16,3,256]{3,1,2,0:T(8,128)(2,1)} %stack.2), calls=%async_computation.2 | async-start | bytes 3145728 | tf_op jit(solution)/shard_map/all_to_all | solution.py:141
  235.4 196.4 %reduce-scatter.2.cloned.1.call-start = ((), (), s32[]{:S(2)}) async-start(), calls=%async_computation.6 | async-start | bytes 10485760 | tf_op jit(solution)/shard_map/reduce_scatter | solution.py:157
  319.1 4.6 copy-start.14
  320.4 3.5 copy-start.3
  332.5 3.7 copy-start.4
  337.1 1.2 copy-start.5
  338.2 3.7 copy-start.9
  340.2 3.0 copy-start.6
  347.8 87.2 %copy-start.13 = (bf16[16,2,128]{2,1,0:T(2,128)(2,1)S(1)}, bf16[16,2,128]{2,1,0:T(2,128)(2,1)}, u32[]{:S(2)}) copy-start(bf16[16,2,128]{2,1,0:T(2,128)(2,1)} %param.29) | copy-start | bytes 24580
  347.8 87.2 %copy-start.8 = (bf16[512,1024]{1,0:T(8,128)(2,1)S(1)}, bf16[512,1024]{1,0:T(8,128)(2,1)}, u32[]{:S(2)}) copy-start(bf16[512,1024]{1,0:T(8,128)(2,1)} %param.28) | copy-start | bytes 3145732
  347.8 137.8 %all-gather.5.cloned.1.call-start = ((), (), s32[]{:S(2)}) async-start(), calls=%async_computation.7 | async-start | bytes 5242880 | tf_op jit(solution)/shard_map/all_gather | solution.py:170
  431.8 47.6 %copy-start.16 = (s32[8]{0:T(128)S(1)}, s32[8]{0:T(128)}, u32[]{:S(2)}) copy-start(s32[8]{0:T(128)} %param.20) | copy-start | bytes 100
  489.2 9.6 %collective-permute-start = (bf16[256,2,128]{2,0,1:T(8,128)(2,1)S(1)}, bf16[256,2,128]{2,0,1:T(8,128)(2,1)S(1)}, u32[]{:S(2)}, u32[]{:S(2)}) collective-permute-start(bf16[256,2,128]{2,0,1:T(8,128)(2,1)S(1)} %slice.86), channel_id=1, source_target_pairs={{0,4},{4,8},{8,12},{12,16},{16,20},{20,24},{24,28},{28,32},{32,36}... | collective-permute-start | bytes 393224 | tf_op jit(solution)/shard_map/ppermute | solution.py:13
  501.0 4.1 copy-start.1
Sparse Core Ops, SparseCore 0:
  209.4 54.9 all-gather.2
  347.9 83.8 reduce-scatter.1
  435.1 50.4 all-gather.4
